TPU v7x, 256 devices: a whole 4x4x8 slice. The times are simulated.
256 devices in a mesh: outer: 8 (over z_hi, y), shard: 32 (over z_lo, x, core).
Axes of the slice: x: 4, y: 4, z: 8 (z_hi: 2, z_lo: 4; z = z_hi * 4 + z_lo), core: 2. Of those that a mesh axis runs over, the one named last changes fastest.
Arguments:
- grad_values: bfloat16 [8, 32, 256, 14848], P('outer', 'shard'), may hold values from -6 to 6
- grad_scales: bfloat16 [8, 32, 256, 116], P('outer', 'shard'), may hold values from 0.029907227 to 0.29882812
- block_owner: int32 [256], replicated, may hold values from 0 to 31, as said below
- projector: bfloat16 [8192, 256], P(('outer', 'shard')), may hold values from -0.375 to 0.375
- weights: bfloat16 [8192, 14848], P(('outer', 'shard')), may hold values from -6 to 6
- first_moment: float32 [256, 14848], P('shard'), may hold values from -6 to 6
- second_moment: float32 [256, 14848], P('shard'), may hold values from 0.5 to 4
Outputs:
- new_weights: bfloat16 [8192, 14848], P(('outer', 'shard'))
- new_first: float32 [256, 14848], P('shard')
- new_second: float32 [256, 14848], P('shard')
Inputs may be any that keep to these rules, and one draw needn't show every extreme that they name: `block_owner`: every index of shard owns exactly 8 rows.
All inputs are finite; a program needn't handle non-finite values.
Results may differ from a plain program's by a relative error of at most 0.0015.
Values may be sent and summed in bfloat16 or wider, within the bound.
A program may use at most 128 MiB of HBM per device.

v0:
```python
import jax
import jax.numpy as jnp
from jax import lax
from jax.sharding import PartitionSpec as P

first_decay = 0.9
second_decay = 0.999
step_count = 100.0
update_scale = 0.25


def per_device(
    grad_values, grad_scales, block_owner, projector, weights, first_moment, second_moment
):
    shards = lax.axis_size("shard")
    rank_rows = block_owner.shape[0]
    owned_rows = rank_rows // shards
    values = grad_values[0, 0]
    scales = grad_scales[0, 0]
    col_blocks = scales.shape[1]
    block_width = values.shape[1] // col_blocks
    row_index = jnp.arange(rank_rows, dtype=jnp.int32)
    sort_keys = block_owner * rank_rows + row_index
    position = jnp.sum((sort_keys[None, :] < sort_keys[:, None]).astype(jnp.int32), axis=1)
    placing = (position[None, :] == row_index[:, None]).astype(jnp.bfloat16)
    sent_values = jnp.dot(placing, values, preferred_element_type=jnp.float32).astype(jnp.bfloat16)
    sent_scales = jnp.dot(placing, scales, preferred_element_type=jnp.float32).astype(jnp.bfloat16)
    got_values, got_scales = (
        lax.all_to_all(
            sent_values.reshape(shards, owned_rows, -1),
            "shard",
            split_axis=0,
            concat_axis=0,
            tiled=True,
        ),
        lax.all_to_all(
            sent_scales.reshape(shards, owned_rows, col_blocks),
            "shard",
            split_axis=0,
            concat_axis=0,
            tiled=True,
        ),
    )
    blocked = got_values.reshape(shards, owned_rows, col_blocks, block_width).astype(jnp.float32)
    pod_sum = jnp.sum(blocked * got_scales.astype(jnp.float32)[..., None], axis=0)
    pod_low = pod_sum.reshape(owned_rows, -1).astype(jnp.bfloat16)
    all_rows = lax.all_gather(pod_low[None], "outer", axis=0, tiled=True)
    owned = jnp.sum(all_rows.astype(jnp.float32), axis=0)
    new_first = first_decay * first_moment + (1.0 - first_decay) * owned
    new_second = second_decay * second_moment + (1.0 - second_decay) * owned * owned
    corrected = new_first / (1.0 - first_decay**step_count)
    spread = jnp.sqrt(new_second / (1.0 - second_decay**step_count)) + 1e-08
    update = (corrected / spread).astype(jnp.bfloat16)
    gathered = lax.all_gather(update, "shard", axis=0, tiled=True)
    reordered = jnp.dot(projector, placing.T, preferred_element_type=jnp.float32).astype(
        jnp.bfloat16
    )
    change = jnp.dot(reordered, gathered, preferred_element_type=jnp.float32)
    new_weights = (weights.astype(jnp.float32) - update_scale * change).astype(jnp.bfloat16)
    return (new_weights, new_first, new_second)


def solution(mesh):
    placed = (
        P("outer", "shard", None, None),
        P("outer", "shard", None, None),
        P(),
        P(("outer", "shard"), None),
        P(("outer", "shard"), None),
        P("shard", None),
        P("shard", None),
    )
    return jax.shard_map(
        per_device,
        mesh=mesh,
        in_specs=placed,
        out_specs=(P(("outer", "shard"), None), P("shard", None), P("shard", None)),
        check_vma=False,
    )
```

profile of v0, /device:TPU:1, one launch (start us, length us, event | category | flops | bytes accessed | tf_op | source)
XLA Modules:
  0.0 366.5 jit_solution(17580511060379455319)
XLA Ops:
  7.2 0.0 copy-start
  7.2 0.7 iota_add_fusion
  7.9 0.2 convert_reduce_fusion.1
  8.1 0.0 copy-done
  8.1 0.2 convolution_convert_fusion.1
  8.3 0.7 copy.13
  9.0 10.0 %all-to-all-start.1 = ((bf16[32,8,116]{2,1,0:T(8,128)(2,1)}), bf16[32,8,116]{2,1,0:T(8,128)(2,1)S(1)}, u32[]{:S(2)}, u32[]{:S(2)}) async-start(bf16[32,8,116]{2,1,0:T(8,128)(2,1)} %bitcast.3), calls=%async_computation.1 | async-start | bytes 131072 | tf_op jit(solution)/shard_map/all_to_all | solution.py:36
  19.0 8.4 %fusion = bf16[32,8,14848]{2,1,0:T(8,128)(2,1)} fusion(bf16[1,1,256,14848]{3,2,1,0:T(8,128)(2,1)} %param.7, s32[256]{0:T(256)S(1)} %convert_reduce_fusion.1), kind=kOutput, calls=%fused_computation.1 | convolution fusion | flops 1950023680 | bytes 15205376 | tf_op jit(solution)/shard_map/dot_general | solution.py:26
  27.4 0.0 all-to-all-done.1
  27.4 7.8 %all-to-all-start = ((bf16[32,8,14848]{2,1,0:T(8,128)(2,1)}), bf16[32,8,14848]{2,1,0:T(8,128)(2,1)}, u32[]{:S(2)}, u32[]{:S(2)}) async-start(bf16[32,8,14848]{2,1,0:T(8,128)(2,1)} %fusion), calls=%async_computation | async-start | bytes 15204352 | tf_op jit(solution)/shard_map/all_to_all | solution.py:29
  35.2 0.0 copy-start.2
  35.2 0.0 all-gather.6.cloned.1.call-start
  35.3 0.4 copy.14
  35.7 0.0 copy-start.1
  35.7 0.0 copy-start.3
  35.7 166.9 %all-to-all-done = bf16[32,8,14848]{2,1,0:T(8,128)(2,1)} async-done(((bf16[32,8,14848]{2,1,0:T(8,128)(2,1)}), bf16[32,8,14848]{2,1,0:T(8,128)(2,1)}, u32[]{:S(2)}, u32[]{:S(2)}) %all-to-all-start) | async-done | bytes 7602208 | tf_op jit(solution)/shard_map/all_to_all | solution.py:29
  202.7 8.6 %fusion.3 = bf16[8,14848]{1,0:T(8,128)(2,1)} fusion(bf16[32,8,14848]{2,1,0:T(8,128)(2,1)} %all-to-all-done, f32[32,8,116]{1,2,0:T(8,128)S(1)} %copy.14), kind=kLoop, calls=%fused_computation.6 | loop fusion | flops 11284480 | bytes 7958528 | tf_op jit(solution)/shard_map/reduce_sum | solution.py:45
  211.2 0.0 all-gather.6.cloned.1.call-update
  211.3 0.0 all-gather.4.cloned.1.call-start
  211.3 71.3 %all-gather.6.cloned.1.call-done = bf16[64,14848]{1,0:T(8,128)(2,1)} async-done(((bf16[8,14848]{1,0:T(8,128)(2,1)}), bf16[64,14848]{1,0:T(8,128)(2,1)}) %all-gather.6.cloned.1.call-update) | async-done | bytes 1900560 | tf_op jit(solution)/shard_map/all_gather | solution.py:47
  282.6 1.8 convert_reduce_fusion
  284.4 0.0 copy-done.2
  284.4 2.2 divide_convert_fusion
  286.6 0.0 all-gather.4.cloned.1.call-update
  286.6 67.3 %all-gather.4.cloned.1.call-done = bf16[256,14848]{1,0:T(8,128)(2,1)} async-done(((bf16[8,14848]{1,0:T(8,128)(2,1)}), bf16[256,14848]{1,0:T(8,128)(2,1)}) %all-gather.4.cloned.1.call-update) | async-done | bytes 7602192 | tf_op jit(solution)/shard_map/all_gather | solution.py:54
  353.9 0.0 copy-done.1
  353.9 0.0 copy-done.3
  353.9 5.7 %fusion.2 = bf16[32,14848]{1,0:T(8,128)(2,1)} fusion(bf16[256,14848]{1,0:T(8,128)(2,1)} %all-gather.4.cloned.1.call-done, bf16[32,14848]{1,0:T(8,128)(2,1)S(1)} %copy-done.1, bf16[32,256]{1,0:T(8,128)(2,1)S(1)} %copy-done.3, s32[256]{0:T(256)S(1)} %convert_reduce_fusion.1), kind=kOutput, calls=%fused_computation.4 | convolution fusion | flops 249438208 | bytes 9520128 | tf_op jit(solution)/shard_map/dot_general | solution.py:58
Async XLA Ops:
  7.2 0.9 copy-start
  9.0 18.4 %all-to-all-start.1 = ((bf16[32,8,116]{2,1,0:T(8,128)(2,1)}), bf16[32,8,116]{2,1,0:T(8,128)(2,1)S(1)}, u32[]{:S(2)}, u32[]{:S(2)}) async-start(bf16[32,8,116]{2,1,0:T(8,128)(2,1)} %bitcast.3), calls=%async_computation.1 | async-start | bytes 131072 | tf_op jit(solution)/shard_map/all_to_all | solution.py:36
  27.4 175.2 %all-to-all-start = ((bf16[32,8,14848]{2,1,0:T(8,128)(2,1)}), bf16[32,8,14848]{2,1,0:T(8,128)(2,1)}, u32[]{:S(2)}, u32[]{:S(2)}) async-start(bf16[32,8,14848]{2,1,0:T(8,128)(2,1)} %fusion), calls=%async_computation | async-start | bytes 15204352 | tf_op jit(solution)/shard_map/all_to_all | solution.py:29
  35.2 249.2 %copy-start.2 = (f32[8,14848]{1,0:T(8,128)S(1)}, f32[8,14848]{1,0:T(8,128)}, u32[]{:S(2)}) copy-start(f32[8,14848]{1,0:T(8,128)} %param.12) | copy-start | bytes 1425412
  35.2 247.3 %all-gather.6.cloned.1.call-start = ((), (), s32[]{:S(2)}) async-start(), calls=%async_computation.3 | async-start | bytes 2138112 | tf_op jit(solution)/shard_map/all_gather | solution.py:47
  35.7 318.2 %copy-start.1 = (bf16[32,14848]{1,0:T(8,128)(2,1)S(1)}, bf16[32,14848]{1,0:T(8,128)(2,1)}, u32[]{:S(2)}) copy-start(bf16[32,14848]{1,0:T(8,128)(2,1)} %param.11) | copy-start | bytes 2850820
  35.7 318.2 %copy-start.3 = (bf16[32,256]{1,0:T(8,128)(2,1)S(1)}, bf16[32,256]{1,0:T(8,128)(2,1)}, u32[]{:S(2)}) copy-start(bf16[32,256]{1,0:T(8,128)(2,1)} %param.10) | copy-start | bytes 49156
  211.3 142.7 %all-gather.4.cloned.1.call-start = ((), (), s32[]{:S(2)}) async-start(), calls=%async_computation.2 | async-start | bytes 7839744 | tf_op jit(solution)/shard_map/all_gather | solution.py:54
Sparse Core Ops, SparseCore 0:
  211.4 71.1 all-gather.5
  286.8 67.1 all-gather.3
where the time goes:
time: 367 us
  waiting for transfers between devices  306 us (83%)
  starting transfers between devices  17.9 us (5%)
  matrix products  14.3 us (4%)
  between operations  14.1 us (4%)
  other arithmetic  13.5 us (4%)
    all_to_all x1, waiting for transfers between devices, per_device(): lax.all_to_all(sent_values.reshape(shards, owned_rows, -1), 'shard', spli...  167 us
    all_gather x1, waiting for transfers between devices, per_device(): all_rows = lax.all_gather(pod_low[None], 'outer', axis=0, tiled=True)  71.3 us
    all_gather x1, waiting for transfers between devices, per_device(): gathered = lax.all_gather(update, 'shard', axis=0, tiled=True)  67.3 us
    all_to_all x1, starting transfers between devices, per_device(): lax.all_to_all(sent_scales.reshape(shards, owned_rows, col_blocks), 'shar...  10 us
    reduce_sum x1, other arithmetic, per_device(): jnp.sum(blocked * got_scales.astype(jnp.float32)[..., None], axis=0)  8.58 us
    dot_general x1, matrix products, per_device(): jnp.dot(placing, values, preferred_element_type=jnp.float32)  8.39 us
    all_to_all x1, starting transfers between devices, per_device(): lax.all_to_all(sent_values.reshape(shards, owned_rows, -1), 'shard', spli...  7.78 us
  transfers between devices with their start and end apart: 4, of which 3 were waited for; matrix products, arithmetic and copies ran while one was open for 2% of the time, Pallas kernels for 0%

commit v1 on v0

v1 whole, which is shorter than its diff:
```python
import functools
import jax
import jax.numpy as jnp
from jax import lax
from jax.experimental import pallas as pl
from jax.experimental.pallas import tpu as pltpu
from jax.sharding import PartitionSpec as P

first_decay = 0.9
second_decay = 0.999
step_count = 100.0
update_scale = 0.25

f32, bf16 = jnp.float32, jnp.bfloat16
MESH = pl.DeviceIdType.MESH

RANK = 256
TILES = 116
HALF = TILES // 2
HC = HALF * 128

PIECES = (
    ("A", 0, 2, -1),
    ("A", 2, 4, -1),
    ("B", 6, 8, -1),
    ("A", 14, 2, -1),
    ("B", 16, 8, 1),
    ("A", 24, 4, 1),
    ("A", 28, 6, -1),
    ("B", 34, 8, 1),
    ("B", 42, 8, -1),
    ("A", 50, 8, 1),
)
ORDER = (
    "0c", "1c", "2c", "0mid", "3c", "4c", "0end", "1mid",
    "5c", "3mid", "6c", "2mid", "7c", "1end", "4mid", "3end",
    "0zsum", "5mid", "8c", "2end", "6mid", "9c", "5end", "1zsum",
    "7mid", "3zsum", "2xsum", "4end", "0ysum", "6end", "8mid", "9mid",
    "5zsum", "1ysum", "2zsum", "0agz", "4xsum", "7end", "8end", "3ysum",
    "5ysum", "0fwd", "9end", "6zsum", "1agz", "2agz", "7xsum", "4zsum",
    "6ysum", "3agz", "0fin", "8xsum", "5agz", "1fwd", "2agx", "3fwd",
    "9zsum", "5fwd", "7zsum", "4agz", "1fin", "3fin", "5fin", "6agz",
    "2fwd", "8zsum", "9ysum", "7agz", "4agx", "6fwd", "2fin", "8agz",
    "7agx", "4fwd", "6fin", "9agz", "8agx", "7fwd", "9fwd", "4fin",
    "8fwd", "9fin", "8fin", "7fin",
)


def messages():
    names = ["sc", "pj", "wb", "m1", "m2"]
    for i, (kind, _, _, _) in enumerate(PIECES):
        names += [f"{i}raw", f"{i}out", f"{i}r1", f"{i}r2", f"{i}r3", f"{i}g1", f"{i}g2", f"{i}g3"]
        names += [f"{i}z{k}" for k in range(1, 8)] + [f"{i}gz{k}" for k in range(1, 8)]
        if kind == "A":
            names += [f"{i}y{k}" for k in range(1, 4)]
            names += [f"{i}o0{z}{c}" for z in range(2) for c in range(2) if z + c]
        else:
            names += [f"{i}x{k}" for k in range(1, 4)] + [f"{i}gx{k}" for k in range(1, 4)]
            names += [
                f"{i}o{y}{z}{c}" for y in range(4) for z in range(2) for c in range(2) if y + z + c
            ]
    return {name: k for k, name in enumerate(names)}


MSG = messages()
LOCAL = {
    name: k
    for k, name in enumerate(
        ["sc", "pj", "wb", "m1", "m2"]
        + [f"{i}{n}" for i in range(len(PIECES)) for n in ("raw", "out", "own")]
    )
}


def scratch():
    v = pltpu.VMEM
    shapes = dict(
        V0=v((RANK, HC), bf16),
        V1=v((RANK, HC), bf16),
        SC0=v((RANK, TILES), bf16),
        SC1=v((RANK, TILES), bf16),
        PJ=v((2, 32, RANK), bf16),
        PL=v((RANK, RANK), bf16),
        PT=v((RANK, RANK), bf16),
        SR0=v((TILES, RANK), bf16),
        SR1=v((TILES, RANK), bf16),
        RE=v((64, RANK), bf16),
        WB=v((2, 32, HC), bf16),
        NW=v((2, 32, HC), bf16),
        M1=v((2, 8, HC), f32),
        M2=v((2, 8, HC), f32),
        S=v((HALF, 4, 4, 16, 128), bf16),
        G=v((HALF, 4, 4, 16, 128), bf16),
        ssem=pltpu.SemaphoreType.DMA((len(MSG),)),
        rsem=pltpu.SemaphoreType.DMA((len(MSG),)),
        lsem=pltpu.SemaphoreType.DMA((len(LOCAL),)),
        near=pltpu.SemaphoreType.REGULAR((3,)),
    )
    for i, (kind, _, w, _) in enumerate(PIECES):
        if kind == "A":
            part, n = (w, 4, 16, 128), w // 2
            shapes[f"X{i}"] = v((w, 4, 16, 128), bf16)
            shapes[f"RY{i}"] = v((4, n, 16, 128), bf16)
        else:
            q = w // 4
            part, n = (q, 4, 4, 16, 128), q // 2
            shapes[f"Y{i}"] = v(part, bf16)
            shapes[f"RX{i}"] = v((4, q, 4, 16, 128), bf16)
            shapes[f"X{i}"] = v((q, 4, 16, 128), bf16)
        for r in ("R1", "R2", "R3", "T"):
            shapes[f"{r}{i}"] = v(part, bf16)
        shapes[f"RZ{i}"] = v((8, n, 16, 128), bf16)
        shapes[f"OW{i}"] = v((2, 8, n * 128), f32)
    return shapes


def kernel(names, owner, vals, scales, proj, weights, m1, m2, out_w, out_o, *refs):
    r = dict(zip(names, refs))
    S, G = r["S"], r["G"]
    o = lax.axis_index("outer")
    s = lax.axis_index("shard")
    c = lax.rem(s, 2)
    x = lax.rem(lax.div(s, 2), 4)
    zl = lax.div(s, 8)
    y = lax.rem(o, 4)
    zh = lax.div(o, 4)
    z = zh * 4 + zl

    def xi(d):
        return lax.rem(x + d + 4, 4)

    def yi(d):
        return lax.rem(y + d + 4, 4)

    def zi(d):
        return lax.rem(z + d + 8, 8)

    def dev(dx=0, dy=0, dz=0, dc=0):
        zz = zi(dz)
        cc = lax.rem(c + dc, 2)
        return (lax.div(zz, 4) * 4 + yi(dy), lax.rem(zz, 4) * 8 + xi(dx) * 2 + cc)

    def col(core, tile):
        return pl.multiple_of(core * HC + tile * 128, 128)

    started = []

    def make(name, src, dst, to):
        k = MSG[name]
        return pltpu.make_async_remote_copy(
            src_ref=src,
            dst_ref=dst,
            send_sem=r["ssem"].at[k],
            recv_sem=r["rsem"].at[k],
            device_id=to,
            device_id_type=MESH,
        )

    def send(name, src, dst, **to):
        copy = make(name, src, dst, dev(**to))
        copy.start()
        started.append(copy)

    def got(name, dst):
        make(name, dst, dst, dev(dc=1)).wait_recv()

    local_copies = {}

    def local(name, src, dst):
        copy = pltpu.make_async_copy(src, dst, r["lsem"].at[LOCAL[name]])
        copy.start()
        local_copies[name] = copy

    def local_wait(name):
        local_copies.pop(name).wait()

    barrier = pltpu.get_barrier_semaphore()
    six = [dict(dx=1), dict(dx=-1), dict(dy=1), dict(dy=-1), dict(dz=1), dict(dz=-1)]
    for to in six + [dict(dc=1)]:
        pl.semaphore_signal(barrier, inc=1, device_id=dev(**to), device_id_type=MESH)

    local("sc", scales, r["SR0"])
    for i, (_, off, w, _) in enumerate(PIECES):
        local(
            f"{i}raw",
            vals.at[:, pl.ds(col(c, off), w * 128)],
            r["V0"].at[:, pl.ds(off * 128, w * 128)],
        )
    local("pj", proj, r["PJ"].at[c])
    local("wb", weights.at[:, pl.ds(col(c, 0), HC)], r["WB"].at[c])
    local("m1", m1.at[:, pl.ds(col(c, 0), HC)], r["M1"].at[c])
    local("m2", m2.at[:, pl.ds(col(c, 0), HC)], r["M2"].at[c])

    pl.semaphore_wait(barrier, 7)
    pc = 1 - c
    send("sc", scales, r["SR1"], dc=1)
    for i, (_, off, w, _) in enumerate(PIECES):
        send(
            f"{i}raw",
            vals.at[:, pl.ds(col(pc, off), w * 128)],
            r["V1"].at[:, pl.ds(off * 128, w * 128)],
            dc=1,
        )
    send("pj", proj, r["PJ"].at[c], dc=1)
    send("m1", m1.at[:, pl.ds(col(pc, 0), HC)], r["M1"].at[c], dc=1)
    send("m2", m2.at[:, pl.ds(col(pc, 0), HC)], r["M2"].at[c], dc=1)
    send("wb", weights.at[:, pl.ds(col(pc, 0), HC)], r["WB"].at[c], dc=1)

    def near_signal(k):
        for to in six if k == 0 else six[4:]:
            pl.semaphore_signal(
                r["near"].at[k], inc=1, device_id=dev(**to), device_id_type=MESH
            )

    def near_wait(k):
        pl.semaphore_wait(r["near"].at[k], 6 if k == 0 else 2)

    near_signal(0)

    rows = lax.broadcasted_iota(jnp.int32, (1, RANK), 1)
    keys = jnp.broadcast_to((owner[...] * RANK + rows).astype(f32), (RANK, RANK))
    keys_t = keys.T
    place = jnp.sum(jnp.where(keys_t < keys, 1.0, 0.0), axis=0, keepdims=True)
    lines = lax.broadcasted_iota(jnp.int32, (RANK, RANK), 0).astype(f32)
    r["PL"][...] = jnp.where(place == lines, 1.0, 0.0).astype(bf16)
    place_t = jnp.sum(jnp.where(keys < keys_t, 1.0, 0.0), axis=1, keepdims=True)
    lanes = lax.broadcasted_iota(jnp.int32, (RANK, RANK), 1).astype(f32)
    r["PT"][...] = jnp.where(place_t == lanes, 1.0, 0.0).astype(bf16)

    def total(terms):
        out = terms[0].astype(f32)
        for term in terms[1:]:
            out = out + term.astype(f32)
        return out

    def compute(i):
        _, off, w, _ = PIECES[i]
        local_wait(f"{i}raw")
        got(f"{i}raw", r["V1"].at[:, pl.ds(off * 128, w * 128)])

        def body(j, carry):
            cols = pl.ds(pl.multiple_of((off + 2 * j) * 128, 256), 256)
            block = lax.broadcasted_iota(jnp.int32, (TILES, 256), 0)
            lane = lax.broadcasted_iota(jnp.int32, (TILES, 256), 1)
            want = c * HALF + off + 2 * j + jnp.where(lane >= 128, 1, 0)
            spread = jnp.where(block == want, 1.0, 0.0).astype(bf16)
            e0 = jnp.dot(r["SC0"][...], spread, preferred_element_type=f32)
            e1 = jnp.dot(r["SC1"][...], spread, preferred_element_type=f32)
            both = r["V0"][:, cols].astype(f32) * e0 + r["V1"][:, cols].astype(f32) * e1
            put = jnp.dot(r["PL"][...], both.astype(bf16), preferred_element_type=f32)
            put = put.astype(bf16)
            S[off + 2 * j] = put[:, :128].reshape(4, 4, 16, 128)
            S[off + 2 * j + 1] = put[:, 128:].reshape(4, 4, 16, 128)
            return carry

        lax.fori_loop(0, w // 2, body, 0)

    def ring(i):
        kind, off, w, sg = PIECES[i]
        if kind == "A":
            return sg, xi, (lambda d: dict(dx=d)), (lambda b, p: b.at[pl.ds(off, w), :, p])
        q = w // 4
        return sg, yi, (lambda d: dict(dy=d)), (lambda b, p: b.at[pl.ds(off + p * q, q)])

    def piece_loop(n, body):
        def step(t, carry):
            body(t)
            return carry

        lax.fori_loop(0, n, step, 0)

    def start(i):
        sg, at, to, part = ring(i)
        send(f"{i}r1", part(S, at(2 * sg)), r[f"R1{i}"], **to(sg))
        send(f"{i}r3", part(S, at(-sg)), r[f"R3{i}"], **to(-sg))

    def own_part(i):
        kind, off, w, _ = PIECES[i]
        if kind == "A":
            return w, lambda p, t: S[off + t, :, p]
        q = w // 4
        return q, lambda p, t: S[off + p * q + t]

    def mid(i):
        sg, at, to, part = ring(i)
        got(f"{i}r1", r[f"R1{i}"])
        n, own = own_part(i)
        p = at(sg)

        def body(t):
            r[f"T{i}"][t] = total([own(p, t), r[f"R1{i}"][t]]).astype(bf16)

        piece_loop(n, body)
        send(f"{i}r2", r[f"T{i}"], r[f"R2{i}"], **to(sg))

    def end(i):
        kind = PIECES[i][0]
        got(f"{i}r3", r[f"R3{i}"])
        got(f"{i}r2", r[f"R2{i}"])
        n, own = own_part(i)
        p = x if kind == "A" else y
        dst = r[f"X{i}"] if kind == "A" else r[f"Y{i}"]

        def body(t):
            dst[t] = total([own(p, t), r[f"R3{i}"][t], r[f"R2{i}"][t]]).astype(bf16)

        piece_loop(n, body)
        if kind == "A":
            z_send(i)
        else:
            for k in range(1, 4):
                send(f"{i}x{k}", dst.at[:, :, xi(k)], r[f"RX{i}"].at[x], dx=k)

    def xsum(i):
        for k in range(1, 4):
            got(f"{i}x{k}", r[f"RX{i}"].at[xi(-k)])

        def body(t):
            terms = [r[f"Y{i}"][t, :, x]] + [r[f"RX{i}"][xi(-k), t] for k in range(1, 4)]
            r[f"X{i}"][t] = total(terms).astype(bf16)

        piece_loop(PIECES[i][2] // 4, body)
        z_send(i)

    def z_tiles(i):
        kind, _, w, _ = PIECES[i]
        return w // 2 if kind == "A" else w // 8

    def z_send(i):
        n = z_tiles(i)
        for k in range(1, 8):
            zz = zi(k)
            src = r[f"X{i}"].at[pl.ds(lax.div(zz, 4) * n, n), lax.rem(zz, 4)]
            send(f"{i}z{k}", src, r[f"RZ{i}"].at[z], dz=k)

    def z_terms(i, t):
        n = z_tiles(i)
        terms = [r[f"X{i}"][zh * n + t, zl]]
        return terms + [r[f"RZ{i}"][zi(-k), t] for k in range(1, 8)]

    def z_got(i):
        for k in range(1, 8):
            got(f"{i}z{k}", r[f"RZ{i}"].at[zi(-k)])

    def first_tile(i, yy, hh):
        kind, off, w, _ = PIECES[i]
        if kind == "A":
            return off + hh * (w // 2)
        return off + yy * (w // 4) + hh * (w // 8)

    def update(i, owned_of):
        n = z_tiles(i)
        tile0 = first_tile(i, y, zh)

        def body(t):
            owned = owned_of(t)
            cols = pl.ds(pl.multiple_of((tile0 + t) * 128, 128), 128)
            dirs = []
            for h in range(2):
                part = owned[8 * h : 8 * h + 8]
                r[f"OW{i}"][h, :, pl.ds(pl.multiple_of(t * 128, 128), 128)] = part
                nf = first_decay * r["M1"][h, :, cols] + (1.0 - first_decay) * part
                ns = second_decay * r["M2"][h, :, cols] + (1.0 - second_decay) * part * part
                corrected = nf / (1.0 - first_decay**step_count)
                spread = jnp.sqrt(ns / (1.0 - second_decay**step_count)) + 1e-08
                dirs.append(corrected / spread)
            G[tile0 + t, zl, x] = jnp.concatenate(dirs, axis=0).astype(bf16)

        piece_loop(n, body)
        mine = G.at[pl.ds(tile0, n), zl, x]
        for k in range(1, 8):
            send(f"{i}gz{k}", mine, mine, dz=k)
        cols = pl.ds(col(c, tile0), n * 128)
        local(f"{i}own", r[f"OW{i}"].at[c], out_o.at[:, cols])
        for dy in range(4 if PIECES[i][0] == "B" else 1):
            for dz in range(2):
                for dc in range(2):
                    if dy + dz + dc:
                        src = r[f"OW{i}"].at[pc if dc else c]
                        send(
                            f"{i}o{dy}{dz}{dc}", src, out_o.at[:, cols], dy=dy, dz=4 * dz, dc=dc
                        )

    def owned_got(i):
        n = z_tiles(i)
        for dy in range(4 if PIECES[i][0] == "B" else 1):
            for dz in range(2):
                for dc in range(2):
                    if dy + dz + dc:
                        tile = first_tile(i, yi(-dy), (1 - zh) if dz else zh)
                        cols = pl.ds(col(pc if dc else c, tile), n * 128)
                        got(f"{i}o{dy}{dz}{dc}", out_o.at[:, cols])

    def zsum_a(i):
        z_got(i)

        def body(t):
            r[f"RY{i}"][y, t] = total(z_terms(i, t)).astype(bf16)

        piece_loop(z_tiles(i), body)
        for k in range(1, 4):
            send(f"{i}y{k}", r[f"RY{i}"].at[y], r[f"RY{i}"].at[y], dy=k)

    def ysum(i):
        for k in range(1, 4):
            got(f"{i}y{k}", r[f"RY{i}"].at[yi(-k)])
        update(i, lambda t: total([r[f"RY{i}"][k, t] for k in range(4)]))

    def zsum_b(i):
        z_got(i)
        update(i, lambda t: total(z_terms(i, t)))

    def gather_z_got(i):
        n = z_tiles(i)
        for k in range(1, 8):
            zz = zi(-k)
            tile = first_tile(i, y, lax.div(zz, 4))
            got(f"{i}gz{k}", G.at[pl.ds(tile, n), lax.rem(zz, 4), x])

    def last_ring(i):
        sg, at, to, part = ring(i)
        mine = part(G, at(0))
        send(f"{i}g1", mine, mine, **to(sg))
        send(f"{i}g3", mine, mine, **to(-sg))

    def agz(i):
        gather_z_got(i)
        kind, off, w, _ = PIECES[i]
        if kind == "A":
            last_ring(i)
        else:
            q = w // 4
            mine = G.at[pl.ds(off + y * q, q), :, x]
            for k in range(1, 4):
                send(f"{i}gx{k}", mine, mine, dx=k)

    def agx(i):
        _, off, w, _ = PIECES[i]
        q = w // 4
        for k in range(1, 4):
            got(f"{i}gx{k}", G.at[pl.ds(off + y * q, q), :, xi(-k)])
        last_ring(i)

    def fwd(i):
        sg, at, to, part = ring(i)
        behind = part(G, at(-sg))
        got(f"{i}g1", behind)
        send(f"{i}g2", behind, behind, **to(sg))

    def fin(i):
        _, off, w, _ = PIECES[i]
        sg, at, to, part = ring(i)
        got(f"{i}g3", part(G, at(sg)))
        got(f"{i}g2", part(G, at(2 * sg)))

        def body(j, carry):
            cols = pl.ds(pl.multiple_of((off + 2 * j) * 128, 256), 256)
            u = jnp.concatenate(
                [G[off + 2 * j].reshape(256, 128), G[off + 2 * j + 1].reshape(256, 128)], axis=1
            )
            change = jnp.dot(r["RE"][...], u, preferred_element_type=f32)
            old = r["WB"][:, :, cols].reshape(64, 256).astype(f32)
            new = (old - update_scale * change).astype(bf16)
            r["NW"][:, :, cols] = new.reshape(2, 32, 256)
            return carry

        lax.fori_loop(0, w // 2, body, 0)
        here = pl.ds(off * 128, w * 128)
        there = pl.ds(col(c, off), w * 128)
        send(f"{i}out", r["NW"].at[pc, :, here], out_w.at[:, there], dc=1)
        local(f"{i}out", r["NW"].at[c, :, here], out_w.at[:, there])

    actions = dict(
        mid=mid, end=end, xsum=xsum, ysum=ysum, agz=agz, agx=agx, fwd=fwd, fin=fin
    )
    local_wait("sc")
    got("sc", r["SR1"])
    for src, dst in (("SR0", "SC0"), ("SR1", "SC1")):
        r[dst][...] = r[src][...].astype(f32).T.astype(bf16)
    computed = 0
    updating = {"A": "ysum", "B": "zsum"}
    have_moments = have_weights = False
    for item in ORDER:
        i, what = int(item[0]), item[1:]
        if what == updating[PIECES[i][0]] and not have_moments:
            have_moments = True
            for name in ("m1", "m2"):
                local_wait(name)
            got("m1", r["M1"].at[pc])
            got("m2", r["M2"].at[pc])
        if what == "fin" and not have_weights:
            have_weights = True
            for name in ("pj", "wb"):
                local_wait(name)
            got("pj", r["PJ"].at[pc])
            got("wb", r["WB"].at[pc])
            reordered = jnp.dot(
                r["PJ"][...].reshape(64, RANK), r["PT"][...], preferred_element_type=f32
            )
            r["RE"][...] = reordered.astype(bf16)
        if what == "c":
            compute(i)
            start(i)
            if computed < 3:
                near_wait(computed)
                if computed < 2:
                    near_signal(computed + 1)
            computed += 1
        elif what == "zsum":
            (zsum_a if PIECES[i][0] == "A" else zsum_b)(i)
        else:
            actions[what](i)

    for i, (_, off, w, _) in enumerate(PIECES):
        owned_got(i)
        got(f"{i}out", out_w.at[:, pl.ds(col(pc, off), w * 128)])
    for name in list(local_copies):
        local_wait(name)
    for copy in started:
        copy.wait_send()


def per_device(
    grad_values, grad_scales, block_owner, projector, weights, first_moment, second_moment
):
    shapes = scratch()
    any_spec = pl.BlockSpec(memory_space=pl.ANY)
    new_weights, owned = pl.pallas_call(
        functools.partial(kernel, tuple(shapes)),
        out_shape=(
            jax.ShapeDtypeStruct(weights.shape, bf16),
            jax.ShapeDtypeStruct(first_moment.shape, f32),
        ),
        in_specs=[pl.BlockSpec(memory_space=pltpu.VMEM)] + [any_spec] * 6,
        out_specs=(any_spec, any_spec),
        scratch_shapes=list(shapes.values()),
        compiler_params=pltpu.CompilerParams(
            collective_id=0, has_side_effects=True, vmem_limit_bytes=60 * 1024 * 1024
        ),
    )(
        block_owner.reshape(1, RANK),
        grad_values[0, 0],
        grad_scales[0, 0].T,
        projector,
        weights,
        first_moment,
        second_moment,
    )
    new_first = first_decay * first_moment + (1.0 - first_decay) * owned
    new_second = second_decay * second_moment + (1.0 - second_decay) * owned * owned
    return (new_weights, new_first, new_second)


def solution(mesh):
    placed = (
        P("outer", "shard", None, None),
        P("outer", "shard", None, None),
        P(),
        P(("outer", "shard"), None),
        P(("outer", "shard"), None),
        P("shard", None),
        P("shard", None),
    )
    return jax.shard_map(
        per_device,
        mesh=mesh,
        in_specs=placed,
        out_specs=(P(("outer", "shard"), None), P("shard", None), P("shard", None)),
        check_vma=False,
    )
```

time: 367 us -> 89.8 us (0.24)
  waiting for transfers between devices: 306 us -> 0 us
  Pallas kernels: 0 us -> 84.6 us
  starting transfers between devices: 17.9 us -> 0 us
  matrix products: 14.3 us -> 0 us
  between operations: 14.1 us -> 0.67 us
  other arithmetic: 13.5 us -> 2.09 us
    all_to_all x2 -> x0, waiting for transfers between devices: 167 us -> none  [the longest x1 167 us: per_device(): lax.all_to_all(sent_values.reshape(shards, owned_rows, -1), 'shard', spli...]
    all_gather x2 -> x0, waiting for transfers between devices: 139 us -> none  [the longest x1 71.3 us: per_device(): all_rows = lax.all_gather(pod_low[None], 'outer', axis=0, tiled=True)]
    pallas_call x0 -> x1, Pallas kernels: none -> 84.6 us  [per_device(): pl.pallas_call(functools.partial(kernel, tuple(shapes)), out_shape=(jax.S...]
    all_to_all x2 -> x0, starting transfers between devices: 17.8 us -> none  [the longest x1 10 us: per_device(): lax.all_to_all(sent_scales.reshape(shards, owned_rows, col_blocks), 'shar...]
    dot_general x3 -> x0, matrix products: 14.3 us -> none  [the longest x1 8.39 us: per_device(): jnp.dot(placing, values, preferred_element_type=jnp.float32)]
    reduce_sum x3 -> x0, other arithmetic: 10.6 us -> none  [the longest x1 8.58 us: per_device(): jnp.sum(blocked * got_scales.astype(jnp.float32)[..., None], axis=0)]
  transfers between devices with their start and end apart: 4 -> 0, of which waited for: 3 -> 0; matrix products, arithmetic and copies ran while one was open for 2% -> 0% of each run, Pallas kernels for 0% -> 0%
where the time goes in v1:
time: 89.8 us; the launch traced here: 89.6 us
  Pallas kernels  84.6 us (94%)
  local copies, waits for them, and re-layouts  2.19 us (2%)
  other arithmetic  2.09 us (2%)
    pallas_call x1, Pallas kernels, per_device(): pl.pallas_call(functools.partial(kernel, tuple(shapes)), out_shape=(jax.S...  84.6 us
    unnamed x5, local copies, waits for them, and re-layouts  2.19 us
    add x1, other arithmetic, per_device(): second_decay * second_moment + (1.0 - second_decay) * owned * owned  2.09 us

profile of v1, /device:TPU:1, one launch (start us, length us, event | category | flops | bytes accessed | tf_op | source)
XLA Modules:
  0.0 89.6 jit_solution(4014549763888060140)
XLA Ops:
  0.6 0.0 copy-start.1
  0.6 0.0 copy-start
  0.7 84.6 %shard_map.94 = (bf16[32,14848]{1,0:T(8,128)(2,1)}, f32[8,14848]{1,0:T(8,128)}) custom-call(s32[1,256]{1,0:T(1,128)} %bitcast.7, bf16[256,14848]{1,0:T(8,128)(2,1)} %bitcast.5, bf16[116,256]{1,0:T(8,128)(2,1)} %bitcast.6, bf16[32,256]{1,0:T(8,128)(2,1)} %proj.1, bf16[32,14848]{1,0:T(8,128)(2,1)} %weights.1, f32[8,14848]{1,0:T(8,128)} %m1.1, f32[8,14848]{1,0:T(8,128)} %m2.1), custom_call_target="tpu_custom_call" | custom-call | tf_op jit(solution)/shard_map/pallas_call | solution.py:528
  85.3 0.0 copy-done.1
  85.3 0.0 copy-done
  85.3 2.1 %fusion = (f32[8,14848]{1,0:T(8,128)}, f32[8,14848]{1,0:T(8,128)}) fusion(f32[8,14848]{1,0:T(8,128)} %get-tuple-element.6, f32[8,14848]{1,0:T(8,128)S(1)} %copy-done.1, f32[8,14848]{1,0:T(8,128)S(1)} %copy-done), kind=kLoop, calls=%fused_computation.1 | loop fusion | flops 831488 | bytes 2375680 | tf_op jit(solution)/shard_map/add | solution.py:550
  87.4 2.2 %copy.11 = bf16[32,14848]{1,0:T(8,128)(2,1)} copy(bf16[32,14848]{1,0:T(8,128)(2,1)} %get-tuple-element.12) | data formatting | bytes 1900544
Async XLA Ops:
  0.6 84.7 %copy-start.1 = (f32[8,14848]{1,0:T(8,128)S(1)}, f32[8,14848]{1,0:T(8,128)}, u32[]{:S(2)}) copy-start(f32[8,14848]{1,0:T(8,128)} %m2.1) | copy-start | bytes 1425412
  0.6 84.7 %copy-start = (f32[8,14848]{1,0:T(8,128)S(1)}, f32[8,14848]{1,0:T(8,128)}, u32[]{:S(2)}) copy-start(f32[8,14848]{1,0:T(8,128)} %m1.1) | copy-start | bytes 1425412

commit v2 on v1

--- a/solution.py
+++ b/solution.py
@@ -1,4 +1,5 @@
 import functools
+import math
 import jax
 import jax.numpy as jnp
 from jax import lax
@@ -46,44 +47,61 @@
 )
 
 
-def messages():
-    names = ["sc", "pj", "wb", "m1", "m2"]
+def keys():
+    names = ["sc", "pj", "wb", "m1", "m2", "o", "out"]
     for i, (kind, _, _, _) in enumerate(PIECES):
-        names += [f"{i}raw", f"{i}out", f"{i}r1", f"{i}r2", f"{i}r3", f"{i}g1", f"{i}g2", f"{i}g3"]
-        names += [f"{i}z{k}" for k in range(1, 8)] + [f"{i}gz{k}" for k in range(1, 8)]
-        if kind == "A":
-            names += [f"{i}y{k}" for k in range(1, 4)]
-            names += [f"{i}o0{z}{c}" for z in range(2) for c in range(2) if z + c]
-        else:
-            names += [f"{i}x{k}" for k in range(1, 4)] + [f"{i}gx{k}" for k in range(1, 4)]
-            names += [
-                f"{i}o{y}{z}{c}" for y in range(4) for z in range(2) for c in range(2) if y + z + c
-            ]
+        names += [f"{i}{n}" for n in ("raw", "r1", "r23", "z", "gz", "g1", "g23")]
+        names += [f"{i}y"] if kind == "A" else [f"{i}x", f"{i}gx"]
     return {name: k for k, name in enumerate(names)}
 
 
-MSG = messages()
-LOCAL = {
-    name: k
-    for k, name in enumerate(
-        ["sc", "pj", "wb", "m1", "m2"]
-        + [f"{i}{n}" for i in range(len(PIECES)) for n in ("raw", "out", "own")]
-    )
-}
+KEYS = keys()
+
+
+def key_of(name):
+    if not name[0].isdigit():
+        return KEYS[name]
+    i, what = name[0], name[1:]
+    if what == "out":
+        return KEYS["out"]
+    if what[0] == "o":
+        return KEYS["o"]
+    pairs = dict(raw="raw", r1="r1", r2="r23", r3="r23", g1="g1", g2="g23", g3="g23")
+    return KEYS[i + pairs.get(what, what[:-1])]
+
+
+def send_group(name):
+    if not name[0].isdigit():
+        return {"sc": "sc", "wb": "wb"}.get(name, "pm")
+    i, what = name[0], name[1:]
+    if what[0] == "o":
+        return "out" if what == "out" else "o"
+    return i + ("big" if what in ("raw", "r1", "r2", "r3", "g1", "g2", "g3") else "small")
+
+
+GROUPS = ["sc", "wb", "pm", "out", "o"]
+GROUPS += [f"{i}{n}" for i in range(len(PIECES)) for n in ("big", "small")]
+GROUPS = {name: k for k, name in enumerate(GROUPS)}
+
+
+def extents(tiles):
+    for bb in (4, 3, 2, 1):
+        for cc in (4, 3, 2, 1):
+            if tiles % (bb * cc) == 0 and tiles // (bb * cc) <= HALF:
+                return tiles // (bb * cc), bb, cc
+    raise ValueError(tiles)
 
 
 def scratch():
     v = pltpu.VMEM
     shapes = dict(
-        V0=v((RANK, HC), bf16),
-        V1=v((RANK, HC), bf16),
+        V=v((2, RANK, HC), bf16),
         SC0=v((RANK, TILES), bf16),
         SC1=v((RANK, TILES), bf16),
         PJ=v((2, 32, RANK), bf16),
         PL=v((RANK, RANK), bf16),
         PT=v((RANK, RANK), bf16),
-        SR0=v((TILES, RANK), bf16),
-        SR1=v((TILES, RANK), bf16),
+        SR=v((2, TILES, RANK), bf16),
         RE=v((64, RANK), bf16),
         WB=v((2, 32, HC), bf16),
         NW=v((2, 32, HC), bf16),
@@ -91,9 +109,8 @@
         M2=v((2, 8, HC), f32),
         S=v((HALF, 4, 4, 16, 128), bf16),
         G=v((HALF, 4, 4, 16, 128), bf16),
-        ssem=pltpu.SemaphoreType.DMA((len(MSG),)),
-        rsem=pltpu.SemaphoreType.DMA((len(MSG),)),
-        lsem=pltpu.SemaphoreType.DMA((len(LOCAL),)),
+        ssem=pltpu.SemaphoreType.DMA((len(GROUPS),)),
+        rsem=pltpu.SemaphoreType.DMA((len(KEYS),)),
         near=pltpu.SemaphoreType.REGULAR((3,)),
     )
     for i, (kind, _, w, _) in enumerate(PIECES):
@@ -107,8 +124,8 @@
             shapes[f"Y{i}"] = v(part, bf16)
             shapes[f"RX{i}"] = v((4, q, 4, 16, 128), bf16)
             shapes[f"X{i}"] = v((q, 4, 16, 128), bf16)
-        for r in ("R1", "R2", "R3", "T"):
-            shapes[f"{r}{i}"] = v(part, bf16)
+        shapes[f"R1{i}"] = shapes[f"T{i}"] = v(part, bf16)
+        shapes[f"R23{i}"] = v((2,) + part, bf16)
         shapes[f"RZ{i}"] = v((8, n, 16, 128), bf16)
         shapes[f"OW{i}"] = v((2, 8, n * 128), f32)
     return shapes
@@ -143,15 +160,14 @@
     def col(core, tile):
         return pl.multiple_of(core * HC + tile * 128, 128)
 
-    started = []
+    sent = {}
 
     def make(name, src, dst, to):
-        k = MSG[name]
         return pltpu.make_async_remote_copy(
             src_ref=src,
             dst_ref=dst,
-            send_sem=r["ssem"].at[k],
-            recv_sem=r["rsem"].at[k],
+            send_sem=r["ssem"].at[GROUPS[send_group(name)]],
+            recv_sem=r["rsem"].at[key_of(name)],
             device_id=to,
             device_id_type=MESH,
         )
@@ -159,32 +175,27 @@
     def send(name, src, dst, **to):
         copy = make(name, src, dst, dev(**to))
         copy.start()
-        started.append(copy)
+        group = send_group(name)
+        size = math.prod(src.shape) * src.dtype.itemsize
+        sent[group] = sent.get(group, 0) + size
 
     def got(name, dst):
-        make(name, dst, dst, dev(dc=1)).wait_recv()
-
-    local_copies = {}
+        pltpu.make_async_copy(dst, dst, r["rsem"].at[key_of(name)]).wait()
 
     def local(name, src, dst):
-        copy = pltpu.make_async_copy(src, dst, r["lsem"].at[LOCAL[name]])
-        copy.start()
-        local_copies[name] = copy
-
-    def local_wait(name):
-        local_copies.pop(name).wait()
+        pltpu.make_async_copy(src, dst, r["rsem"].at[key_of(name)]).start()
 
     barrier = pltpu.get_barrier_semaphore()
     six = [dict(dx=1), dict(dx=-1), dict(dy=1), dict(dy=-1), dict(dz=1), dict(dz=-1)]
     for to in six + [dict(dc=1)]:
         pl.semaphore_signal(barrier, inc=1, device_id=dev(**to), device_id_type=MESH)
 
-    local("sc", scales, r["SR0"])
+    local("sc", scales, r["SR"].at[0])
     for i, (_, off, w, _) in enumerate(PIECES):
         local(
             f"{i}raw",
             vals.at[:, pl.ds(col(c, off), w * 128)],
-            r["V0"].at[:, pl.ds(off * 128, w * 128)],
+            r["V"].at[0, :, pl.ds(off * 128, w * 128)],
         )
     local("pj", proj, r["PJ"].at[c])
     local("wb", weights.at[:, pl.ds(col(c, 0), HC)], r["WB"].at[c])
@@ -193,12 +204,12 @@
 
     pl.semaphore_wait(barrier, 7)
     pc = 1 - c
-    send("sc", scales, r["SR1"], dc=1)
+    send("sc", scales, r["SR"].at[1], dc=1)
     for i, (_, off, w, _) in enumerate(PIECES):
         send(
             f"{i}raw",
             vals.at[:, pl.ds(col(pc, off), w * 128)],
-            r["V1"].at[:, pl.ds(off * 128, w * 128)],
+            r["V"].at[1, :, pl.ds(off * 128, w * 128)],
             dc=1,
         )
     send("pj", proj, r["PJ"].at[c], dc=1)
@@ -235,8 +246,7 @@
 
     def compute(i):
         _, off, w, _ = PIECES[i]
-        local_wait(f"{i}raw")
-        got(f"{i}raw", r["V1"].at[:, pl.ds(off * 128, w * 128)])
+        got(f"{i}raw", r["V"].at[:, :, pl.ds(off * 128, w * 128)])
 
         def body(j, carry):
             cols = pl.ds(pl.multiple_of((off + 2 * j) * 128, 256), 256)
@@ -246,7 +256,7 @@
             spread = jnp.where(block == want, 1.0, 0.0).astype(bf16)
             e0 = jnp.dot(r["SC0"][...], spread, preferred_element_type=f32)
             e1 = jnp.dot(r["SC1"][...], spread, preferred_element_type=f32)
-            both = r["V0"][:, cols].astype(f32) * e0 + r["V1"][:, cols].astype(f32) * e1
+            both = r["V"][0, :, cols].astype(f32) * e0 + r["V"][1, :, cols].astype(f32) * e1
             put = jnp.dot(r["PL"][...], both.astype(bf16), preferred_element_type=f32)
             put = put.astype(bf16)
             S[off + 2 * j] = put[:, :128].reshape(4, 4, 16, 128)
@@ -272,7 +282,7 @@
     def start(i):
         sg, at, to, part = ring(i)
         send(f"{i}r1", part(S, at(2 * sg)), r[f"R1{i}"], **to(sg))
-        send(f"{i}r3", part(S, at(-sg)), r[f"R3{i}"], **to(-sg))
+        send(f"{i}r3", part(S, at(-sg)), r[f"R23{i}"].at[1], **to(-sg))
 
     def own_part(i):
         kind, off, w, _ = PIECES[i]
@@ -291,18 +301,17 @@
             r[f"T{i}"][t] = total([own(p, t), r[f"R1{i}"][t]]).astype(bf16)
 
         piece_loop(n, body)
-        send(f"{i}r2", r[f"T{i}"], r[f"R2{i}"], **to(sg))
+        send(f"{i}r2", r[f"T{i}"], r[f"R23{i}"].at[0], **to(sg))
 
     def end(i):
         kind = PIECES[i][0]
-        got(f"{i}r3", r[f"R3{i}"])
-        got(f"{i}r2", r[f"R2{i}"])
+        got(f"{i}r3", r[f"R23{i}"])
         n, own = own_part(i)
         p = x if kind == "A" else y
         dst = r[f"X{i}"] if kind == "A" else r[f"Y{i}"]
 
         def body(t):
-            dst[t] = total([own(p, t), r[f"R3{i}"][t], r[f"R2{i}"][t]]).astype(bf16)
+            dst[t] = total([own(p, t), r[f"R23{i}"][0, t], r[f"R23{i}"][1, t]]).astype(bf16)
 
         piece_loop(n, body)
         if kind == "A":
@@ -312,8 +321,7 @@
                 send(f"{i}x{k}", dst.at[:, :, xi(k)], r[f"RX{i}"].at[x], dx=k)
 
     def xsum(i):
-        for k in range(1, 4):
-            got(f"{i}x{k}", r[f"RX{i}"].at[xi(-k)])
+        got(f"{i}x1", r[f"RX{i}"].at[pl.ds(0, 3)])
 
         def body(t):
             terms = [r[f"Y{i}"][t, :, x]] + [r[f"RX{i}"][xi(-k), t] for k in range(1, 4)]
@@ -339,8 +347,7 @@
         return terms + [r[f"RZ{i}"][zi(-k), t] for k in range(1, 8)]
 
     def z_got(i):
-        for k in range(1, 8):
-            got(f"{i}z{k}", r[f"RZ{i}"].at[zi(-k)])
+        got(f"{i}z1", r[f"RZ{i}"].at[pl.ds(0, 7)])
 
     def first_tile(i, yy, hh):
         kind, off, w, _ = PIECES[i]
@@ -371,7 +378,7 @@
         for k in range(1, 8):
             send(f"{i}gz{k}", mine, mine, dz=k)
         cols = pl.ds(col(c, tile0), n * 128)
-        local(f"{i}own", r[f"OW{i}"].at[c], out_o.at[:, cols])
+        local(f"{i}o000", r[f"OW{i}"].at[c], out_o.at[:, cols])
         for dy in range(4 if PIECES[i][0] == "B" else 1):
             for dz in range(2):
                 for dc in range(2):
@@ -381,16 +388,6 @@
                             f"{i}o{dy}{dz}{dc}", src, out_o.at[:, cols], dy=dy, dz=4 * dz, dc=dc
                         )
 
-    def owned_got(i):
-        n = z_tiles(i)
-        for dy in range(4 if PIECES[i][0] == "B" else 1):
-            for dz in range(2):
-                for dc in range(2):
-                    if dy + dz + dc:
-                        tile = first_tile(i, yi(-dy), (1 - zh) if dz else zh)
-                        cols = pl.ds(col(pc if dc else c, tile), n * 128)
-                        got(f"{i}o{dy}{dz}{dc}", out_o.at[:, cols])
-
     def zsum_a(i):
         z_got(i)
 
@@ -402,8 +399,7 @@
             send(f"{i}y{k}", r[f"RY{i}"].at[y], r[f"RY{i}"].at[y], dy=k)
 
     def ysum(i):
-        for k in range(1, 4):
-            got(f"{i}y{k}", r[f"RY{i}"].at[yi(-k)])
+        got(f"{i}y1", r[f"RY{i}"].at[pl.ds(0, 3)])
         update(i, lambda t: total([r[f"RY{i}"][k, t] for k in range(4)]))
 
     def zsum_b(i):
@@ -411,11 +407,8 @@
         update(i, lambda t: total(z_terms(i, t)))
 
     def gather_z_got(i):
-        n = z_tiles(i)
-        for k in range(1, 8):
-            zz = zi(-k)
-            tile = first_tile(i, y, lax.div(zz, 4))
-            got(f"{i}gz{k}", G.at[pl.ds(tile, n), lax.rem(zz, 4), x])
+        a, bb, cc = extents(7 * z_tiles(i))
+        got(f"{i}gz1", S.at[pl.ds(0, a), pl.ds(0, bb), pl.ds(0, cc)])
 
     def last_ring(i):
         sg, at, to, part = ring(i)
@@ -437,8 +430,7 @@
     def agx(i):
         _, off, w, _ = PIECES[i]
         q = w // 4
-        for k in range(1, 4):
-            got(f"{i}gx{k}", G.at[pl.ds(off + y * q, q), :, xi(-k)])
+        got(f"{i}gx1", G.at[pl.ds(off, q), :, pl.ds(0, 3)])
         last_ring(i)
 
     def fwd(i):
@@ -450,8 +442,10 @@
     def fin(i):
         _, off, w, _ = PIECES[i]
         sg, at, to, part = ring(i)
-        got(f"{i}g3", part(G, at(sg)))
-        got(f"{i}g2", part(G, at(2 * sg)))
+        if PIECES[i][0] == "A":
+            got(f"{i}g3", G.at[pl.ds(off, w), :, pl.ds(0, 2)])
+        else:
+            got(f"{i}g3", G.at[pl.ds(off, w // 2)])
 
         def body(j, carry):
             cols = pl.ds(pl.multiple_of((off + 2 * j) * 128, 256), 256)
@@ -473,10 +467,9 @@
     actions = dict(
         mid=mid, end=end, xsum=xsum, ysum=ysum, agz=agz, agx=agx, fwd=fwd, fin=fin
     )
-    local_wait("sc")
-    got("sc", r["SR1"])
-    for src, dst in (("SR0", "SC0"), ("SR1", "SC1")):
-        r[dst][...] = r[src][...].astype(f32).T.astype(bf16)
+    got("sc", r["SR"])
+    for k in range(2):
+        r[f"SC{k}"][...] = r["SR"][k].astype(f32).T.astype(bf16)
     computed = 0
     updating = {"A": "ysum", "B": "zsum"}
     have_moments = have_weights = False
@@ -484,16 +477,12 @@
         i, what = int(item[0]), item[1:]
         if what == updating[PIECES[i][0]] and not have_moments:
             have_moments = True
-            for name in ("m1", "m2"):
-                local_wait(name)
-            got("m1", r["M1"].at[pc])
-            got("m2", r["M2"].at[pc])
+            got("m1", r["M1"])
+            got("m2", r["M2"])
         if what == "fin" and not have_weights:
             have_weights = True
-            for name in ("pj", "wb"):
-                local_wait(name)
-            got("pj", r["PJ"].at[pc])
-            got("wb", r["WB"].at[pc])
+            got("pj", r["PJ"])
+            got("wb", r["WB"])
             reordered = jnp.dot(
                 r["PJ"][...].reshape(64, RANK), r["PT"][...], preferred_element_type=f32
             )
@@ -511,13 +500,15 @@
         else:
             actions[what](i)
 
-    for i, (_, off, w, _) in enumerate(PIECES):
-        owned_got(i)
-        got(f"{i}out", out_w.at[:, pl.ds(col(pc, off), w * 128)])
-    for name in list(local_copies):
-        local_wait(name)
-    for copy in started:
-        copy.wait_send()
+    got("o", out_o)
+    got("out", out_w)
+    for group, size in sent.items():
+        if group == "sc":
+            whole = r["SR"].at[0]
+        else:
+            a, bb, cc = extents(size // 4096)
+            whole = S.at[pl.ds(0, a), pl.ds(0, bb), pl.ds(0, cc)]
+        pltpu.make_async_copy(whole, whole, r["ssem"].at[GROUPS[group]]).wait()
 
 
 def per_device(

time: 89.8 us -> 83.1 us (0.925)
  Pallas kernels: 84.6 us -> 78 us
    pallas_call x1, Pallas kernels: 84.6 us -> 78 us  [per_device(): pl.pallas_call(functools.partial(kernel, tuple(shapes)), out_shape=(jax.S...]
where the time goes in v2:
time: 83.1 us; the launch traced here: 82.9 us
  Pallas kernels  78 us (94%)
  local copies, waits for them, and re-layouts  2.19 us (3%)
  other arithmetic  2.09 us (3%)
    pallas_call x1, Pallas kernels, per_device(): pl.pallas_call(functools.partial(kernel, tuple(shapes)), out_shape=(jax.S...  78 us
    unnamed x5, local copies, waits for them, and re-layouts  2.19 us
    add x1, other arithmetic, per_device(): second_decay * second_moment + (1.0 - second_decay) * owned * owned  2.09 us

profile of v2, /device:TPU:1, one launch (start us, length us, event | category | flops | bytes accessed | tf_op | source)
XLA Modules:
  0.0 82.9 jit_solution(5342004764478033320)
XLA Ops:
  0.6 0.0 copy-start.1
  0.6 0.0 copy-start
  0.7 78.0 %shard_map.94 = (bf16[32,14848]{1,0:T(8,128)(2,1)}, f32[8,14848]{1,0:T(8,128)}) custom-call(s32[1,256]{1,0:T(1,128)} %bitcast.7, bf16[256,14848]{1,0:T(8,128)(2,1)} %bitcast.5, bf16[116,256]{1,0:T(8,128)(2,1)} %bitcast.6, bf16[32,256]{1,0:T(8,128)(2,1)} %proj.1, bf16[32,14848]{1,0:T(8,128)(2,1)} %weights.1, f32[8,14848]{1,0:T(8,128)} %m1.1, f32[8,14848]{1,0:T(8,128)} %m2.1), custom_call_target="tpu_custom_call" | custom-call | tf_op jit(solution)/shard_map/pallas_call | solution.py:519
  78.7 0.0 copy-done.1
  78.7 0.0 copy-done
  78.7 2.1 %fusion = (f32[8,14848]{1,0:T(8,128)}, f32[8,14848]{1,0:T(8,128)}) fusion(f32[8,14848]{1,0:T(8,128)} %get-tuple-element.6, f32[8,14848]{1,0:T(8,128)S(1)} %copy-done.1, f32[8,14848]{1,0:T(8,128)S(1)} %copy-done), kind=kLoop, calls=%fused_computation.1 | loop fusion | flops 831488 | bytes 2375680 | tf_op jit(solution)/shard_map/add | solution.py:541
  80.8 2.2 %copy.11 = bf16[32,14848]{1,0:T(8,128)(2,1)} copy(bf16[32,14848]{1,0:T(8,128)(2,1)} %get-tuple-element.12) | data formatting | bytes 1900544
Async XLA Ops:
  0.6 78.0 %copy-start.1 = (f32[8,14848]{1,0:T(8,128)S(1)}, f32[8,14848]{1,0:T(8,128)}, u32[]{:S(2)}) copy-start(f32[8,14848]{1,0:T(8,128)} %m2.1) | copy-start | bytes 1425412
  0.6 78.0 %copy-start = (f32[8,14848]{1,0:T(8,128)S(1)}, f32[8,14848]{1,0:T(8,128)}, u32[]{:S(2)}) copy-start(f32[8,14848]{1,0:T(8,128)} %m1.1) | copy-start | bytes 1425412

commit v3 on v2

--- a/solution.py
+++ b/solution.py
@@ -19,31 +19,30 @@
 TILES = 116
 HALF = TILES // 2
 HC = HALF * 128
+FAR_FIRST = (4, 3, 5, 2, 6, 1, 7)
 
 PIECES = (
-    ("A", 0, 2, -1),
-    ("A", 2, 4, -1),
-    ("B", 6, 8, -1),
-    ("A", 14, 2, -1),
-    ("B", 16, 8, 1),
-    ("A", 24, 4, 1),
-    ("A", 28, 6, -1),
-    ("B", 34, 8, 1),
+    ("A", 0, 4, 1),
+    ("B", 4, 8, 1),
+    ("B", 12, 8, 1),
+    ("A", 20, 4, 1),
+    ("A", 24, 6, 1),
+    ("B", 30, 8, -1),
+    ("A", 38, 4, -1),
     ("B", 42, 8, -1),
-    ("A", 50, 8, 1),
+    ("A", 50, 8, -1),
 )
 ORDER = (
-    "0c", "1c", "2c", "0mid", "3c", "4c", "0end", "1mid",
-    "5c", "3mid", "6c", "2mid", "7c", "1end", "4mid", "3end",
-    "0zsum", "5mid", "8c", "2end", "6mid", "9c", "5end", "1zsum",
-    "7mid", "3zsum", "2xsum", "4end", "0ysum", "6end", "8mid", "9mid",
-    "5zsum", "1ysum", "2zsum", "0agz", "4xsum", "7end", "8end", "3ysum",
-    "5ysum", "0fwd", "9end", "6zsum", "1agz", "2agz", "7xsum", "4zsum",
-    "6ysum", "3agz", "0fin", "8xsum", "5agz", "1fwd", "2agx", "3fwd",
-    "9zsum", "5fwd", "7zsum", "4agz", "1fin", "3fin", "5fin", "6agz",
-    "2fwd", "8zsum", "9ysum", "7agz", "4agx", "6fwd", "2fin", "8agz",
-    "7agx", "4fwd", "6fin", "9agz", "8agx", "7fwd", "9fwd", "4fin",
-    "8fwd", "9fin", "8fin", "7fin",
+    "0c", "1c", "2c", "3c", "0mid", "4c", "1mid", "5c",
+    "3mid", "6c", "0end", "2mid", "7c", "4mid", "1end", "3end",
+    "6mid", "5mid", "8c", "0zsum", "4end", "7mid", "2end", "6end",
+    "1xsum", "3zsum", "5end", "8mid", "0ysum", "2xsum", "7end", "3ysum",
+    "4zsum", "5xsum", "6zsum", "1zsum", "8end", "0agz", "2zsum", "7xsum",
+    "4ysum", "3agz", "5zsum", "1agz", "0fwd", "6ysum", "8zsum", "3fwd",
+    "2agz", "7zsum", "1agx", "0fin", "4agz", "8ysum", "5agz", "3fin",
+    "6agz", "2agx", "7agz", "1fwd", "4fwd", "5agx", "6fwd", "2fwd",
+    "8agz", "7agx", "1fin", "4fin", "6fin", "5fwd", "8fwd", "7fwd",
+    "2fin", "5fin", "8fin", "7fin",
 )
 
 
@@ -336,7 +335,7 @@
 
     def z_send(i):
         n = z_tiles(i)
-        for k in range(1, 8):
+        for k in FAR_FIRST:
             zz = zi(k)
             src = r[f"X{i}"].at[pl.ds(lax.div(zz, 4) * n, n), lax.rem(zz, 4)]
             send(f"{i}z{k}", src, r[f"RZ{i}"].at[z], dz=k)
@@ -375,8 +374,12 @@
 
         piece_loop(n, body)
         mine = G.at[pl.ds(tile0, n), zl, x]
-        for k in range(1, 8):
+        for k in FAR_FIRST:
             send(f"{i}gz{k}", mine, mine, dz=k)
+
+    def owned_send(i):
+        n = z_tiles(i)
+        tile0 = first_tile(i, y, zh)
         cols = pl.ds(col(c, tile0), n * 128)
         local(f"{i}o000", r[f"OW{i}"].at[c], out_o.at[:, cols])
         for dy in range(4 if PIECES[i][0] == "B" else 1):
@@ -438,6 +441,7 @@
         behind = part(G, at(-sg))
         got(f"{i}g1", behind)
         send(f"{i}g2", behind, behind, **to(sg))
+        owned_send(i)
 
     def fin(i):
         _, off, w, _ = PIECES[i]
@@ -470,7 +474,7 @@
     got("sc", r["SR"])
     for k in range(2):
         r[f"SC{k}"][...] = r["SR"][k].astype(f32).T.astype(bf16)
-    computed = 0
+    rounds = 0
     updating = {"A": "ysum", "B": "zsum"}
     have_moments = have_weights = False
     for item in ORDER:
@@ -490,15 +494,16 @@
         if what == "c":
             compute(i)
             start(i)
-            if computed < 3:
-                near_wait(computed)
-                if computed < 2:
-                    near_signal(computed + 1)
-            computed += 1
         elif what == "zsum":
             (zsum_a if PIECES[i][0] == "A" else zsum_b)(i)
         else:
             actions[what](i)
+
+        if rounds < 3:
+            near_wait(rounds)
+            if rounds < 2:
+                near_signal(rounds + 1)
+        rounds += 1
 
     got("o", out_o)
     got("out", out_w)
@@ -509,6 +514,13 @@
             a, bb, cc = extents(size // 4096)
             whole = S.at[pl.ds(0, a), pl.ds(0, bb), pl.ds(0, cc)]
         pltpu.make_async_copy(whole, whole, r["ssem"].at[GROUPS[group]]).wait()
+
+
+def moments_kernel(weights, owned, first, second, new_weights, new_first, new_second):
+    new_weights[...] = weights[...]
+    grad = owned[...]
+    new_first[...] = first_decay * first[...] + (1.0 - first_decay) * grad
+    new_second[...] = second_decay * second[...] + (1.0 - second_decay) * grad * grad
 
 
 def per_device(
@@ -537,8 +549,22 @@
         first_moment,
         second_moment,
     )
-    new_first = first_decay * first_moment + (1.0 - first_decay) * owned
-    new_second = second_decay * second_moment + (1.0 - second_decay) * owned * owned
+    steps = 2
+    width = first_moment.shape[1] // steps
+
+    def column_block(array):
+        return pl.BlockSpec((array.shape[0], width), lambda j: (0, j))
+
+    ins = (new_weights, owned, first_moment, second_moment)
+    outs = (new_weights, first_moment, second_moment)
+    new_weights, new_first, new_second = pl.pallas_call(
+        moments_kernel,
+        grid=(steps,),
+        out_shape=tuple(jax.ShapeDtypeStruct(a.shape, a.dtype) for a in outs),
+        in_specs=[column_block(a) for a in ins],
+        out_specs=tuple(column_block(a) for a in outs),
+        cost_estimate=pl.CostEstimate(flops=800000, bytes_accessed=4300000, transcendentals=0),
+    )(*ins)
     return (new_weights, new_first, new_second)
 
 

time: 83.1 us -> 76.6 us (0.922)
  Pallas kernels: 78 us -> 75.8 us
  local copies, waits for them, and re-layouts: 2.19 us -> 0 us
  other arithmetic: 2.09 us -> 0 us
    pallas_call x1, Pallas kernels: 78 us -> 73.2 us  [per_device(): pl.pallas_call(functools.partial(kernel, tuple(shapes)), out_shape=(jax.S...]
    pallas_call x0 -> x1, Pallas kernels: none -> 2.63 us  [per_device(): pl.pallas_call(moments_kernel, grid=(steps,), out_shape=tuple((jax.ShapeD...]
    unnamed x5 -> x0, local copies, waits for them, and re-layouts: 2.19 us -> none
    add x1 -> x0, other arithmetic: 2.09 us -> none  [per_device(): second_decay * second_moment + (1.0 - second_decay) * owned * owned]
where the time goes in v3:
time: 76.6 us; the launch traced here: 76.5 us
  Pallas kernels  75.8 us (99%)
    pallas_call x1, Pallas kernels, per_device(): pl.pallas_call(functools.partial(kernel, tuple(shapes)), out_shape=(jax.S...  73.2 us
    pallas_call x1, Pallas kernels, per_device(): pl.pallas_call(moments_kernel, grid=(steps,), out_shape=tuple((jax.ShapeD...  2.63 us

profile of v3, /device:TPU:1, one launch (start us, length us, event | category | flops | bytes accessed | tf_op | source)
XLA Modules:
  0.0 76.5 jit_solution(9742765993964185021)
XLA Ops:
  0.6 73.2 %shard_map.94 = (bf16[32,14848]{1,0:T(8,128)(2,1)}, f32[8,14848]{1,0:T(8,128)}) custom-call(s32[1,256]{1,0:T(1,128)} %bitcast.7, bf16[256,14848]{1,0:T(8,128)(2,1)} %bitcast.5, bf16[116,256]{1,0:T(8,128)(2,1)} %bitcast.6, bf16[32,256]{1,0:T(8,128)(2,1)} %proj.1, bf16[32,14848]{1,0:T(8,128)(2,1)} %weights.1, f32[8,14848]{1,0:T(8,128)} %first.1, f32[8,14848]{1,0:T(8,128)} %second.1), custom_call_target="tpu_custom_call" | custom-call | tf_op jit(solution)/shard_map/pallas_call | solution.py:531
  73.8 2.6 %shard_map.95 = (bf16[32,14848]{1,0:T(8,128)(2,1)}, f32[8,14848]{1,0:T(8,128)}, f32[8,14848]{1,0:T(8,128)}) custom-call(bf16[32,14848]{1,0:T(8,128)(2,1)} %get-tuple-element.5.weights, f32[8,14848]{1,0:T(8,128)} %get-tuple-element.6.owned, f32[8,14848]{1,0:T(8,128)} %first.1, f32[8,14848]{1,0:T(8,128)} %second.1), custom_call_target="tpu_custom_call" | custom-call | flops 800000 | bytes 4300000 | tf_op jit(solution)/shard_map/pallas_call | solution.py:560
